TPU v7x, 32 devices: a whole 2x2x4 slice. The times are simulated.
32 devices in a mesh: ctx: 8 (over z, y), wsh: 4 (over x, core).
Axes of the slice: x: 2, y: 2, z: 4, core: 2. Of those that a mesh axis runs over, the one named last changes fastest.
Arguments:
- tokens: bfloat16 [4, 1024, 2048], P('wsh', 'ctx'), may hold values from -6 to 6
- out_grad: bfloat16 [4, 1024, 2048], P('wsh', 'ctx'), may hold values from -6 to 6
- attn_weight: bfloat16 [4, 2048, 2048], P(None, None, 'wsh'), may hold values from -0.125 to 0.125
- mlp_weight: bfloat16 [3, 2048, 8192], P(None, None, 'wsh'), may hold values from -0.125 to 0.125
- norm_gains: bfloat16 [4, 2048], P(None, 'wsh'), may hold values from 0.25 to 1.75
- adapt_model: bfloat16 [11, 64, 2048], P(None, None, 'wsh'), may hold values from -0.125 to 0.125
- adapt_hidden: bfloat16 [3, 64, 8192], P(None, None, 'wsh'), may hold values from -0.0625 to 0.0625
- lengths: int32 [4], replicated, may hold values from 512 to 1024, as said below
- adapter_pick: int32 [4], replicated, may hold values from 0 to 3
- block_order: int32 [4, 16], P('wsh'), may hold values from 0 to 15, as said below
Outputs:
- layer_out: bfloat16 [4, 1024, 2048], P('wsh', 'ctx')
- input_grad: float32 [4, 1024, 2048], P('wsh', 'ctx')
- adapt_model_grad: float32 [11, 64, 2048], P(None, None, 'wsh')
- adapt_hidden_grad: float32 [3, 64, 8192], P(None, None, 'wsh')
Inputs may be any that keep to these rules, and one draw needn't show every extreme that they name: `lengths`: some sequence has exactly 1024 valid tokens. Each row of block_order is a permutation of the 16 blocks; the two blocks stored on one index of ctx are p and 15 - p for some p, in either order.
All inputs are finite; a program needn't handle non-finite values.
Results may differ from a plain program's by a relative error of at most 0.017.
Values may be sent and summed in bfloat16 or wider, within the bound.
No kernel may reach another device: no remote copies, remote signals or barrier semaphores. Data moves between devices by JAX's collectives and lax.ppermute only.
A program may use at most 512 MiB of HBM per device.

v0:
```python
import jax
import jax.numpy as jnp
from jax import lax
from jax.sharding import PartitionSpec as P

HEADS = 16
HEAD_DIM = 128
FF = 8192
RANK = 16
ADAPTERS = 4
NORM_EPS = 1e-06
ADAPTER_SCALE = 4.0
ROPE_BASE = 500000.0


def rms_scale(values):
    return lax.rsqrt(jnp.mean(values * values, axis=-1, keepdims=True) + NORM_EPS)


def norm_back(values, scale_rows, upstream):
    return scale_rows * upstream - values * scale_rows**3 * jnp.mean(
        upstream * values, axis=-1, keepdims=True
    )


def rotary_tables(positions, head_dim):
    half_dim = head_dim // 2
    frequency = ROPE_BASE ** (-(jnp.arange(half_dim, dtype=jnp.float32) * 2.0) / head_dim)
    angles = positions.astype(jnp.float32)[:, None] * frequency[None, :]
    return (jnp.cos(angles)[:, None, :], jnp.sin(angles)[:, None, :])


def rotate(values, tables, heads_total):
    cosine, sine_part = tables
    row_count = values.shape[0]
    shaped = values.reshape(row_count, heads_total, -1)
    half_dim = shaped.shape[-1] // 2
    first_half = shaped[..., :half_dim]
    second_half = shaped[..., half_dim:]
    turned = jnp.concatenate(
        [
            first_half * cosine - second_half * sine_part,
            second_half * cosine + first_half * sine_part,
        ],
        axis=-1,
    )
    return turned.reshape(row_count, -1)


def rotate_back(gradient, tables, heads_total):
    cosine, sine_part = tables
    row_count = gradient.shape[0]
    shaped = gradient.reshape(row_count, heads_total, -1)
    half_dim = shaped.shape[-1] // 2
    first_half = shaped[..., :half_dim]
    second_half = shaped[..., half_dim:]
    turned = jnp.concatenate(
        [
            first_half * cosine + second_half * sine_part,
            second_half * cosine - first_half * sine_part,
        ],
        axis=-1,
    )
    return turned.reshape(row_count, -1)


def pick_rows(stacked, onehot, adapters):
    part_count, col_count = (stacked.shape[0], stacked.shape[2])
    split_view = stacked.reshape(part_count, adapters, -1, col_count)
    return jnp.einsum(
        "kard,a->krd", split_view, onehot.astype(stacked.dtype), preferred_element_type=jnp.float32
    ).astype(stacked.dtype)


def per_device(
    tokens,
    out_grad,
    attn_weight,
    mlp_weight,
    norm_gains,
    adapt_model,
    adapt_hidden,
    lengths,
    adapter_pick,
    block_order,
):
    input_rows = tokens[0]
    row_count, model_dim = input_rows.shape
    block_rows = row_count // 2
    ctx_size = lax.axis_size("ctx")
    slot_rows = row_count * ctx_size
    heads_all = HEADS
    head_dim = HEAD_DIM
    adapters = ADAPTERS
    score_scale = head_dim ** (-0.5)
    seq_index = lax.axis_index("wsh")
    ctx_index = lax.axis_index("ctx")
    seq_length = lax.dynamic_index_in_dim(lengths, seq_index, keepdims=False)
    chosen = lax.dynamic_index_in_dim(adapter_pick, seq_index, keepdims=False)
    onehot = (jnp.arange(adapters) == chosen).astype(jnp.float32)
    all_positions = (
        block_order[0][:, None] * block_rows + jnp.arange(block_rows)[None, :]
    ).reshape(-1)
    own_positions = lax.dynamic_slice_in_dim(all_positions, ctx_index * row_count, row_count)
    valid_rows = (own_positions < seq_length).astype(jnp.float32)[:, None]
    tables = rotary_tables(own_positions, head_dim)
    key_allowed = (all_positions[None, :] <= own_positions[:, None]) & (
        all_positions[None, :] < seq_length
    )

    def heads_view(matrix):
        return matrix.reshape(matrix.shape[0], heads_all, head_dim)

    attn_full, gains_full, adapt_full = (
        lax.all_gather(attn_weight, "wsh", axis=2, tiled=True),
        lax.all_gather(norm_gains, "wsh", axis=1, tiled=True),
        lax.all_gather(adapt_model, "wsh", axis=2, tiled=True),
    )
    gain_rows = gains_full.astype(jnp.float32)
    model_reduced = pick_rows(adapt_full, onehot, adapters)
    projected_rows = jnp.einsum(
        "td,kde->kte", input_rows, attn_full[:3], preferred_element_type=jnp.float32
    )
    low_in = jnp.einsum(
        "td,krd->ktr", input_rows, model_reduced[:3], preferred_element_type=jnp.float32
    ).astype(jnp.bfloat16)
    projected_rows = projected_rows + ADAPTER_SCALE * jnp.einsum(
        "ktr,krd->ktd", low_in, model_reduced[6:9], preferred_element_type=jnp.float32
    )
    query_scale = rms_scale(projected_rows[0])
    key_scale = rms_scale(projected_rows[1])
    queries = rotate(projected_rows[0] * query_scale * gain_rows[0], tables, heads_all).astype(
        jnp.bfloat16
    )
    own_keys = rotate(projected_rows[1] * key_scale * gain_rows[1], tables, heads_all).astype(
        jnp.bfloat16
    )
    own_values = projected_rows[2].astype(jnp.bfloat16)
    all_keys, all_values = (
        lax.all_gather(own_keys, "ctx", axis=0, tiled=True),
        lax.all_gather(own_values, "ctx", axis=0, tiled=True),
    )
    query_heads = heads_view(queries)
    key_heads = heads_view(all_keys)
    value_heads = heads_view(all_values)
    scores = (
        jnp.einsum("thd,shd->hts", query_heads, key_heads, preferred_element_type=jnp.float32)
        * score_scale
    )
    scores = jnp.where(key_allowed[None], scores, -jnp.inf)
    row_max = jnp.max(scores, axis=-1, keepdims=True)
    log_full = row_max + jnp.log(jnp.sum(jnp.exp(scores - row_max), axis=-1, keepdims=True))
    weights = jnp.exp(scores - log_full).astype(jnp.bfloat16)
    attended = (
        jnp.einsum("hts,shd->thd", weights, value_heads, preferred_element_type=jnp.float32)
        .reshape(row_count, model_dim)
        .astype(jnp.bfloat16)
    )
    log_totals = log_full[..., 0]
    reduced_output = jnp.einsum(
        "td,rd->tr", attended, model_reduced[3], preferred_element_type=jnp.float32
    ).astype(jnp.bfloat16)
    branch = jnp.dot(
        attended, attn_full[3], preferred_element_type=jnp.float32
    ) + ADAPTER_SCALE * jnp.dot(
        reduced_output, model_reduced[9], preferred_element_type=jnp.float32
    )
    branch_scale = rms_scale(branch)
    hidden_in = input_rows.astype(jnp.float32) + branch * branch_scale * gain_rows[2]
    hidden_low = hidden_in.astype(jnp.bfloat16)
    reduced_gate_up = jnp.einsum(
        "td,krd->ktr", hidden_low, model_reduced[4:6], preferred_element_type=jnp.float32
    ).astype(jnp.bfloat16)

    def gate_up_parts(weight_piece, gathered_rows):
        gate_part = jnp.dot(
            hidden_low, weight_piece[0], preferred_element_type=jnp.float32
        ) + ADAPTER_SCALE * jnp.dot(
            reduced_gate_up[0], gathered_rows[0], preferred_element_type=jnp.float32
        )
        up_part = jnp.dot(
            hidden_low, weight_piece[1], preferred_element_type=jnp.float32
        ) + ADAPTER_SCALE * jnp.dot(
            reduced_gate_up[1], gathered_rows[1], preferred_element_type=jnp.float32
        )
        return (gate_part, up_part)

    weight_piece = lax.all_gather(mlp_weight, "wsh", axis=2, tiled=True)
    adapt_piece = lax.all_gather(adapt_hidden, "wsh", axis=2, tiled=True)
    gathered_rows = pick_rows(adapt_piece, onehot, adapters)
    gate_part, up_part = gate_up_parts(weight_piece, gathered_rows)
    product = (jax.nn.silu(gate_part) * up_part).astype(jnp.bfloat16)
    down_total_sum = jnp.einsum(
        "tn,dn->td", product, weight_piece[2], preferred_element_type=jnp.float32
    )
    low_down_sum = jnp.einsum(
        "tn,rn->tr", product, gathered_rows[2], preferred_element_type=jnp.float32
    )
    down_total_sum, low_down_sum = (down_total_sum, low_down_sum)
    low_down = low_down_sum.astype(jnp.bfloat16)
    feedforward_output = down_total_sum + ADAPTER_SCALE * jnp.dot(
        low_down, model_reduced[10], preferred_element_type=jnp.float32
    )
    mlp_scale = rms_scale(feedforward_output)
    result = hidden_in + feedforward_output * mlp_scale * gain_rows[3]
    upstream = out_grad[0].astype(jnp.float32) * valid_rows
    grad_mlp_out = norm_back(feedforward_output, mlp_scale, upstream * gain_rows[3]).astype(
        jnp.bfloat16
    )
    grad_low_down = (
        ADAPTER_SCALE
        * jnp.einsum(
            "td,rd->tr", grad_mlp_out, model_reduced[10], preferred_element_type=jnp.float32
        )
    ).astype(jnp.bfloat16)
    gradient_down_factor = ADAPTER_SCALE * jnp.einsum(
        "tr,td->rd", low_down, grad_mlp_out, preferred_element_type=jnp.float32
    )
    weight_piece = lax.all_gather(mlp_weight, "wsh", axis=2, tiled=True)
    adapt_piece = lax.all_gather(adapt_hidden, "wsh", axis=2, tiled=True)
    gathered_rows = pick_rows(adapt_piece, onehot, adapters)
    gate_part, up_part = gate_up_parts(weight_piece, gathered_rows)
    sigmoid_gate = jax.nn.sigmoid(gate_part)
    silu_gate = gate_part * sigmoid_gate
    product = (silu_gate * up_part).astype(jnp.bfloat16)
    grad_product = jnp.dot(
        grad_mlp_out, weight_piece[2], preferred_element_type=jnp.float32
    ) + jnp.dot(grad_low_down, gathered_rows[2], preferred_element_type=jnp.float32)
    grad_gate = (
        grad_product * up_part * sigmoid_gate * (1.0 + gate_part * (1.0 - sigmoid_gate))
    ).astype(jnp.bfloat16)
    grad_up = (grad_product * silu_gate).astype(jnp.bfloat16)
    input_sum = jnp.einsum(
        "tn,dn->td", grad_gate, weight_piece[0], preferred_element_type=jnp.float32
    ) + jnp.einsum("tn,dn->td", grad_up, weight_piece[1], preferred_element_type=jnp.float32)
    reduced_sum = ADAPTER_SCALE * jnp.stack(
        [
            jnp.einsum(
                "tn,rn->tr", grad_gate, gathered_rows[0], preferred_element_type=jnp.float32
            ),
            jnp.einsum("tn,rn->tr", grad_up, gathered_rows[1], preferred_element_type=jnp.float32),
        ]
    )
    piece_grads = jnp.stack(
        [
            ADAPTER_SCALE
            * jnp.einsum(
                "tr,tn->rn", reduced_gate_up[0], grad_gate, preferred_element_type=jnp.float32
            ),
            ADAPTER_SCALE
            * jnp.einsum(
                "tr,tn->rn", reduced_gate_up[1], grad_up, preferred_element_type=jnp.float32
            ),
            jnp.einsum("tr,tn->rn", grad_low_down, product, preferred_element_type=jnp.float32),
        ]
    )
    input_sum, reduced_sum, picked_hidden = (input_sum, reduced_sum, piece_grads)
    low_grads = reduced_sum.astype(jnp.bfloat16)
    grad_hidden = (
        upstream
        + input_sum
        + jnp.einsum(
            "ktr,krd->td", low_grads, model_reduced[4:6], preferred_element_type=jnp.float32
        )
    )
    grad_a_gate_up = jnp.einsum(
        "ktr,td->krd", low_grads, hidden_low, preferred_element_type=jnp.float32
    )
    grad_branch = norm_back(branch, branch_scale, grad_hidden * gain_rows[2]).astype(jnp.bfloat16)
    grad_low_out = (
        ADAPTER_SCALE
        * jnp.einsum("td,rd->tr", grad_branch, model_reduced[9], preferred_element_type=jnp.float32)
    ).astype(jnp.bfloat16)
    gradient_output_factor = ADAPTER_SCALE * jnp.einsum(
        "tr,td->rd", reduced_output, grad_branch, preferred_element_type=jnp.float32
    )
    grad_a_out = jnp.einsum("tr,td->rd", grad_low_out, attended, preferred_element_type=jnp.float32)
    grad_attended = (
        jnp.einsum("te,de->td", grad_branch, attn_full[3], preferred_element_type=jnp.float32)
        + jnp.einsum(
            "tr,rd->td", grad_low_out, model_reduced[3], preferred_element_type=jnp.float32
        )
    ).astype(jnp.bfloat16)
    grad_heads = heads_view(grad_attended)
    scores = (
        jnp.einsum("thd,shd->hts", query_heads, key_heads, preferred_element_type=jnp.float32)
        * score_scale
    )
    scores = jnp.where(key_allowed[None], scores, -jnp.inf)
    weights_full = jnp.exp(scores - log_totals[..., None])
    grad_probs = jnp.einsum(
        "thd,shd->hts", grad_heads, value_heads, preferred_element_type=jnp.float32
    )
    row_delta = jnp.sum(weights_full * grad_probs, axis=-1, keepdims=True)
    grad_scores = (weights_full * (grad_probs - row_delta)).astype(jnp.bfloat16)
    grad_queries = (
        jnp.einsum("hts,shd->thd", grad_scores, key_heads, preferred_element_type=jnp.float32)
        * score_scale
    ).reshape(row_count, model_dim)
    key_full = (
        jnp.einsum("hts,thd->shd", grad_scores, query_heads, preferred_element_type=jnp.float32)
        * score_scale
    ).reshape(slot_rows, model_dim)
    value_full = jnp.einsum(
        "hts,thd->shd",
        weights_full.astype(jnp.bfloat16),
        grad_heads,
        preferred_element_type=jnp.float32,
    ).reshape(slot_rows, model_dim)
    grad_keys, grad_values = (
        lax.psum_scatter(key_full, "ctx", scatter_dimension=0, tiled=True),
        lax.psum_scatter(value_full, "ctx", scatter_dimension=0, tiled=True),
    )
    grad_proj_query = norm_back(
        projected_rows[0], query_scale, rotate_back(grad_queries, tables, heads_all) * gain_rows[0]
    ).astype(jnp.bfloat16)
    grad_proj_key = norm_back(
        projected_rows[1], key_scale, rotate_back(grad_keys, tables, heads_all) * gain_rows[1]
    ).astype(jnp.bfloat16)
    grad_proj = jnp.stack([grad_proj_query, grad_proj_key, grad_values.astype(jnp.bfloat16)])
    grad_low_qkv = (
        ADAPTER_SCALE
        * jnp.einsum(
            "ktd,krd->ktr", grad_proj, model_reduced[6:9], preferred_element_type=jnp.float32
        )
    ).astype(jnp.bfloat16)
    gradient_projection_factor = ADAPTER_SCALE * jnp.einsum(
        "ktr,ktd->krd", low_in, grad_proj, preferred_element_type=jnp.float32
    )
    grad_a_qkv = jnp.einsum(
        "ktr,td->krd", grad_low_qkv, input_rows, preferred_element_type=jnp.float32
    )
    grad_inputs = (
        grad_hidden
        + jnp.einsum("kte,kde->td", grad_proj, attn_full[:3], preferred_element_type=jnp.float32)
        + jnp.einsum(
            "ktr,krd->td", grad_low_qkv, model_reduced[:3], preferred_element_type=jnp.float32
        )
    )
    picked_model = jnp.concatenate(
        [
            grad_a_qkv,
            grad_a_out[None],
            grad_a_gate_up,
            gradient_projection_factor,
            gradient_output_factor[None],
            gradient_down_factor[None],
        ],
        axis=0,
    )
    spread_model = (onehot[None, :, None, None] * picked_model[:, None]).reshape(
        picked_model.shape[0], adapters * RANK, model_dim
    )
    spread_hidden = (onehot[None, :, None, None] * picked_hidden[:, None]).reshape(
        picked_hidden.shape[0], adapters * RANK, FF
    )
    shard_model, shard_hidden = (
        lax.psum_scatter(spread_model, "wsh", scatter_dimension=2, tiled=True),
        lax.psum_scatter(spread_hidden, "wsh", scatter_dimension=2, tiled=True),
    )
    model_grads, hidden_grads_out = lax.psum((shard_model, shard_hidden), "ctx")
    return (result.astype(jnp.bfloat16)[None], grad_inputs[None], model_grads, hidden_grads_out)


def solution(mesh):
    in_specs = (
        P("wsh", "ctx", None),
        P("wsh", "ctx", None),
        P(None, None, "wsh"),
        P(None, None, "wsh"),
        P(None, "wsh"),
        P(None, None, "wsh"),
        P(None, None, "wsh"),
        P(),
        P(),
        P("wsh", None),
    )
    out_specs = (
        P("wsh", "ctx", None),
        P("wsh", "ctx", None),
        P(None, None, "wsh"),
        P(None, None, "wsh"),
    )
    return jax.shard_map(
        per_device, mesh=mesh, in_specs=in_specs, out_specs=out_specs, check_vma=False
    )
```

profile of v0, /device:TPU:0, one launch (start us, length us, event | category | flops | bytes accessed | tf_op | source)
XLA Modules:
  0.0 1708.9 jit_solution(13489928325962978200)
XLA Ops:
  7.9 11.5 copy.32
  20.4 6.4 all_gather.26
  29.2 10.2 all-gather.10.cloned.1.call-done
  39.4 4.8 fusion.19
  45.8 196.8 %all-gather.8.cloned.1.call-done = bf16[4,2048,2048]{1,2,0:T(8,128)(2,1)} async-done(((bf16[4,2048,512]{1,2,0:T(8,128)(2,1)}), bf16[4,2048,2048]{1,2,0:T(8,128)(2,1)}) %all-gather.8.cloned.1.call-update) | async-done | bytes 33554448 | tf_op jit(solution)/shard_map/all_gather | solution.py:115
  242.6 11.9 fusion.74
  257.7 2.8 copy.34
  260.4 2.5 copy.35
  268.2 2.1 copy.36
  272.9 6.7 fusion.17
  281.4 67.9 %all-gather.12.cloned.1.call-done = bf16[1024,2048]{0,1:T(8,128)(2,1)} async-done(((bf16[128,2048]{0,1:T(8,128)(2,1)}), bf16[1024,2048]{0,1:T(8,128)(2,1)}) %all-gather.12.cloned.1.call-update) | async-done | bytes 4194320 | tf_op jit(solution)/shard_map/all_gather | solution.py:140
  349.3 4.3 fusion.14
  353.6 2.5 exponential_reduce_fusion
  356.9 67.7 %all-gather.18.cloned.1.call-done = bf16[1,1024,2048]{1,2,0:T(8,128)(2,1)} async-done(((bf16[1,128,2048]{1,2,0:T(8,128)(2,1)}), bf16[1,1024,2048]{1,2,0:T(8,128)(2,1)}) %all-gather.18.cloned.1.call-update) | async-done | bytes 4194320 | tf_op jit(solution)/shard_map/all_gather | solution.py:141
  424.6 7.2 convolution_convert_fusion
  432.0 9.3 fusion.13
  442.3 565.8 %all-gather.14.cloned.1.call-done = bf16[3,2048,8192]{2,1,0:T(8,128)(2,1)} async-done(((bf16[3,2048,2048]{2,1,0:T(8,128)(2,1)}), bf16[3,2048,8192]{2,1,0:T(8,128)(2,1)}) %all-gather.14.cloned.1.call-update) | async-done | bytes 100663312 | tf_op jit(solution)/shard_map/all_gather | solution.py:188
  1008.1 15.0 fusion.1
  1023.1 5.0 fusion.8
  1028.1 15.2 fusion.3
  1043.3 7.1 multiply_convert_fusion.3
  1052.2 15.8 fusion.5
  1070.0 15.2 fusion.4
  1085.2 7.1 multiply_convert_fusion.1
  1093.6 16.7 fusion
  1110.4 17.0 fusion.37
  1130.7 4.6 fusion.12
  1136.0 8.2 multiply_reduce_fusion
  1144.2 2.6 multiply_convert_fusion
  1146.8 4.7 broadcast_multiply_fusion
  1151.6 9.4 fusion.81
  1163.0 2.2 fusion.10
  1165.7 3.4 bitcast_multiply_fusion
  1169.1 4.8 fusion.45
  1173.9 125.7 %reduce-scatter.5.cloned.1.call-done = f32[128,2048]{0,1:T(8,128)} async-done(((f32[1024,2048]{0,1:T(8,128)}), f32[128,2048]{0,1:T(8,128)}) %reduce-scatter.5.cloned.1.call-update) | async-done | bytes 1048592 | tf_op jit(solution)/shard_map/reduce_scatter | solution.py:311
  1299.6 2.1 fusion.98
  1306.7 2.7 copy.41
  1309.4 3.0 pad_maximum_fusion.3
  1312.4 2.5 copy.46
  1316.9 133.3 %reduce-scatter.7.cloned.1.call-done = f32[128,2048]{0,1:T(8,128)} async-done(((f32[1024,2048]{0,1:T(8,128)}), f32[128,2048]{0,1:T(8,128)}) %reduce-scatter.7.cloned.1.call-update) | async-done | bytes 1048592 | tf_op jit(solution)/shard_map/reduce_scatter | solution.py:312
  1451.5 2.1 fusion.65
  1457.0 3.3 bitcast_multiply_fusion.1
  1460.4 49.5 %reduce-scatter.11.cloned.1.call-done = f32[3,64,2048]{2,1,0:T(8,128)} async-done(((f32[3,64,8192]{2,1,0:T(8,128)}), f32[3,64,2048]{2,1,0:T(8,128)}) %reduce-scatter.11.cloned.1.call-update) | async-done | bytes 1572880 | tf_op jit(solution)/shard_map/reduce_scatter | solution.py:359
  1509.8 57.0 %reduce-scatter.9.cloned.1.call-done = f32[11,64,512]{2,1,0:T(8,128)} async-done(((f32[11,64,2048]{2,1,0:T(8,128)}), f32[11,64,512]{2,1,0:T(8,128)}) %reduce-scatter.9.cloned.1.call-update) | async-done | bytes 1441808 | tf_op jit(solution)/shard_map/reduce_scatter | solution.py:358
  1568.1 11.3 fusion.32
  1579.4 117.3 %all-reduce.3.cloned.1.call-done = (f32[11,64,512]{2,1,0:T(8,128)}, f32[3,64,2048]{2,1,0:T(8,128)}) async-done(((f32[11,64,512]{2,1,0:T(8,128)}, f32[3,64,2048]{2,1,0:T(8,128)}), (f32[11,64,512]{2,1,0:T(8,128)}, f32[3,64,2048]{2,1,0:T(8,128)})) %all-reduce.3.cloned.1.call-update) | async-done | bytes 3014672 | tf_op jit(solution)/shard_map/psum | solution.py:361
  1696.7 2.6 copy.86
  1699.3 2.7 copy.87
  (214 shorter events, 44.5 us)
Async XLA Ops:
  7.2 32.2 %all-gather.10.cloned.1.call-start = ((), (), s32[]{:S(2)}) async-start(), calls=%async_computation.5 | async-start | bytes 3604480 | tf_op jit(solution)/shard_map/all_gather | solution.py:117
  7.9 234.7 %all-gather.8.cloned.1.call-start = ((), (), s32[]{:S(2)}) async-start(), calls=%async_computation.4 | async-start | bytes 41943040 | tf_op jit(solution)/shard_map/all_gather | solution.py:115
  19.5 7.4 copy-start.58
  19.5 8.8 copy-start.59
  19.5 253.4 %all-gather.16.cloned.1.call-start = ((), (), s32[]{:S(2)}) async-start(), calls=%async_computation.8 | async-start | bytes 3932160 | tf_op jit(solution)/shard_map/all_gather | solution.py:189
  20.2 329.1 %all-gather.12.cloned.1.call-start = ((), (), s32[]{:S(2)}) async-start(), calls=%async_computation.6 | async-start | bytes 4718592 | tf_op jit(solution)/shard_map/all_gather | solution.py:140
  26.9 236.9 %copy-start.42 = (f32[1,2048]{1,0:T(1,128)}, f32[1,2048]{1,0:T(1,128)S(1)}, u32[]{:S(2)}) copy-start(f32[1,2048]{1,0:T(1,128)S(1)} %get-tuple-element.38) | copy-start | bytes 24580
  26.9 238.3 %copy-start.44 = (f32[1,2048]{1,0:T(1,128)}, f32[1,2048]{1,0:T(1,128)S(1)}, u32[]{:S(2)}) copy-start(f32[1,2048]{1,0:T(1,128)S(1)} %get-tuple-element.39) | copy-start | bytes 24580
  29.1 236.3 %copy-start.32 = (f32[128,64]{1,0:T(8,128)}, f32[128,64]{1,0:T(8,128)S(1)}, u32[]{:S(2)}) copy-start(f32[128,64]{1,0:T(8,128)S(1)} %get-tuple-element.40) | copy-start | bytes 98308
  29.1 236.3 %copy-start.34 = (f32[128,64]{1,0:T(8,128)}, f32[128,64]{1,0:T(8,128)S(1)}, u32[]{:S(2)}) copy-start(f32[128,64]{1,0:T(8,128)S(1)} %get-tuple-element.41) | copy-start | bytes 98308
  39.4 6.1 copy-start.4
  45.8 208.7 %copy-start.46 = (bf16[3,16,128]{2,1,0:T(8,128)(2,1)}, bf16[3,16,128]{2,1,0:T(8,128)(2,1)S(1)}, u32[]{:S(2)}) copy-start(bf16[3,16,128]{2,1,0:T(8,128)(2,1)S(1)} %convolution_convert_fusion.1) | copy-start | bytes 36868
  256.1 14.3 copy-start.1
  270.3 154.3 %all-gather.18.cloned.1.call-start = ((), (), s32[]{:S(2)}) async-start(), calls=%async_computation.13 | async-start | bytes 4718592 | tf_op jit(solution)/shard_map/all_gather | solution.py:141
  271.3 736.9 %all-gather.14.cloned.1.call-start = ((), (), s32[]{:S(2)}) async-start(), calls=%async_computation.7 | async-start | bytes 125829120 | tf_op jit(solution)/shard_map/all_gather | solution.py:188
  271.8 1027.7 %reduce-scatter.5.cloned.1.call-start = ((), (), s32[]{:S(2)}) async-start(), calls=%async_computation.9 | async-start | bytes 9437184 | tf_op jit(solution)/shard_map/reduce_scatter | solution.py:311
  272.9 76.4 %copy-start.20 = (bf16[128,16,64]{2,0,1:T(8,128)(2,1)S(1)}, bf16[128,16,64]{2,0,1:T(8,128)(2,1)}, u32[]{:S(2)}) copy-start(bf16[128,16,64]{2,0,1:T(8,128)(2,1)} %get-tuple-element.24) | copy-start | bytes 786436
  272.9 76.4 %copy-start.22 = (bf16[128,16,64]{2,0,1:T(8,128)(2,1)S(1)}, bf16[128,16,64]{2,0,1:T(8,128)(2,1)}, u32[]{:S(2)}) copy-start(bf16[128,16,64]{2,0,1:T(8,128)(2,1)} %get-tuple-element.25) | copy-start | bytes 786436
  424.6 7.2 copy-start.13
  431.8 9.6 copy-start.28
  432.0 9.4 copy-start.48
  432.0 9.8 copy-start.5
  442.1 586.1 %copy-start.14 = (bf16[128,2048]{1,0:T(8,128)(2,1)}, bf16[128,2048]{1,0:T(8,128)(2,1)S(1)}, u32[]{:S(2)}) copy-start(bf16[128,2048]{1,0:T(8,128)(2,1)S(1)} %fusion.68) | copy-start | bytes 1572868
  1050.5 17.5 %copy-start.7 = (bf16[128,8192]{1,0:T(8,128)(2,1)}, bf16[128,8192]{1,0:T(8,128)(2,1)S(1)}, u32[]{:S(2)}) copy-start(bf16[128,8192]{1,0:T(8,128)(2,1)S(1)} %get-tuple-element.54) | copy-start | bytes 6291460
  1052.2 15.8 copy-start.30
  1085.2 7.1 copy-start.24
  1092.3 18.1 %copy-start.11 = (bf16[128,8192]{1,0:T(8,128)(2,1)}, bf16[128,8192]{1,0:T(8,128)(2,1)S(1)}, u32[]{:S(2)}) copy-start(bf16[128,8192]{1,0:T(8,128)(2,1)S(1)} %get-tuple-element.14) | copy-start | bytes 6291460
  1093.6 16.8 copy-start.31
  1130.4 4.9 copy-start.18
  1136.0 8.2 slice-start
  1136.0 8.2 slice-start.1
  1151.6 298.6 %reduce-scatter.7.cloned.1.call-start = ((), (), s32[]{:S(2)}) async-start(), calls=%async_computation.10 | async-start | bytes 9437184 | tf_op jit(solution)/shard_map/reduce_scatter | solution.py:312
  1161.0 348.8 %reduce-scatter.11.cloned.1.call-start = ((), (), s32[]{:S(2)}) async-start(), calls=%async_computation.12 | async-start | bytes 7864320 | tf_op jit(solution)/shard_map/reduce_scatter | solution.py:359
  1169.1 397.7 %reduce-scatter.9.cloned.1.call-start = ((), (), s32[]{:S(2)}) async-start(), calls=%async_computation.11 | async-start | bytes 7208960 | tf_op jit(solution)/shard_map/reduce_scatter | solution.py:358
  1173.9 129.5 %copy-start.33 = (f32[128,64]{1,0:T(8,128)S(1)}, f32[128,64]{1,0:T(8,128)}, u32[]{:S(2)}) copy-start(f32[128,64]{1,0:T(8,128)} %copy-done.32) | copy-start | bytes 98308
  1173.9 129.5 %copy-start.35 = (f32[128,64]{1,0:T(8,128)S(1)}, f32[128,64]{1,0:T(8,128)}, u32[]{:S(2)}) copy-start(f32[128,64]{1,0:T(8,128)} %copy-done.34) | copy-start | bytes 98308
  1306.7 8.2 copy-start.2
  1306.7 8.2 copy-start.43
  1306.7 8.2 copy-start.45
  1312.4 139.1 %copy-start.51 = (f32[128]{0:T(128)S(1)}, f32[128]{0:T(128)}, u32[]{:S(2)}) copy-start(f32[128]{0:T(128)} %copy-done.50) | copy-start | bytes 1540
  1312.4 139.1 %copy-start.53 = (f32[128]{0:T(128)S(1)}, f32[128]{0:T(128)}, u32[]{:S(2)}) copy-start(f32[128]{0:T(128)} %copy-done.52) | copy-start | bytes 1540
  1312.4 139.1 %copy-start.55 = (f32[128]{0:T(128)S(1)}, f32[128]{0:T(128)}, u32[]{:S(2)}) copy-start(f32[128]{0:T(128)} %get-tuple-element.44) | copy-start | bytes 1540
  1312.4 139.1 %copy-start.56 = (f32[128]{0:T(128)S(1)}, f32[128]{0:T(128)}, u32[]{:S(2)}) copy-start(f32[128]{0:T(128)} %get-tuple-element.62) | copy-start | bytes 1540
  1460.3 107.8 %copy-start.27 = (f32[128,2048]{1,0:T(8,128)S(1)}, f32[128,2048]{1,0:T(8,128)}, u32[]{:S(2)}) copy-start(f32[128,2048]{1,0:T(8,128)} %copy-done.26) | copy-start | bytes 3145732
  1460.3 107.8 %copy-start.37 = (bf16[1,128,2048]{1,2,0:T(8,128)(2,1)S(1)}, bf16[1,128,2048]{1,2,0:T(8,128)(2,1)}, u32[]{:S(2)}) copy-start(bf16[1,128,2048]{1,2,0:T(8,128)(2,1)} %copy-done.36) | copy-start | bytes 1572868
  1460.3 107.8 %copy-start.39 = (bf16[1,128,2048]{1,2,0:T(8,128)(2,1)S(1)}, bf16[1,128,2048]{1,2,0:T(8,128)(2,1)}, u32[]{:S(2)}) copy-start(bf16[1,128,2048]{1,2,0:T(8,128)(2,1)} %copy-done.38) | copy-start | bytes 1572868
  1460.3 107.8 %copy-start.41 = (bf16[1,128,2048]{1,2,0:T(8,128)(2,1)S(1)}, bf16[1,128,2048]{1,2,0:T(8,128)(2,1)}, u32[]{:S(2)}) copy-start(bf16[1,128,2048]{1,2,0:T(8,128)(2,1)} %copy-done.40) | copy-start | bytes 1572868
  1460.3 236.4 %all-reduce.3.cloned.1.call-start = ((), (), s32[]{:S(2)}) async-start(), calls=%async_computation.14 | async-start | bytes 6029312 | tf_op jit(solution)/shard_map/psum | solution.py:361
  (25 other events, 65.0 us)
Sparse Core Ops, SparseCore 0:
  9.5 29.8 all-gather.9
  41.0 201.5 all-gather.7
  244.1 28.4 all-gather.15
  274.6 74.6 all-gather.11
  351.8 72.8 all-gather.17
  426.0 582.0 all-gather.13
  1151.7 147.8 reduce-scatter.4
  1303.2 146.9 reduce-scatter.6
  1452.7 57.0 reduce-scatter.10
  1512.2 54.5 reduce-scatter.8
  1570.6 126.0 all-reduce.2
where the time goes:
time: 1720 us; the launch traced here: 1710 us
  waiting for transfers between devices  1390 us (81%)
  matrix products  217 us (13%)
  local copies, waits for them, and re-layouts  42.7 us (2%)
  other arithmetic  33.2 us (2%)
    all_gather x1, waiting for transfers between devices, per_device(): weight_piece = lax.all_gather(mlp_weight, 'wsh', axis=2, tiled=True)  566 us
    all_gather x1, waiting for transfers between devices, per_device(): lax.all_gather(attn_weight, 'wsh', axis=2, tiled=True)  197 us
    reduce_scatter x1, waiting for transfers between devices, per_device(): lax.psum_scatter(value_full, 'ctx', scatter_dimension=0, tiled=True)  133 us
    reduce_scatter x1, waiting for transfers between devices, per_device(): lax.psum_scatter(key_full, 'ctx', scatter_dimension=0, tiled=True)  126 us
    psum x1, waiting for transfers between devices, per_device(): model_grads, hidden_grads_out = lax.psum((shard_model, shard_hidden), 'ctx')  117 us
    all_gather x1, waiting for transfers between devices, per_device(): lax.all_gather(own_keys, 'ctx', axis=0, tiled=True)  67.9 us
    all_gather x1, waiting for transfers between devices, per_device(): lax.all_gather(own_values, 'ctx', axis=0, tiled=True)  67.7 us
    reduce_scatter x1, waiting for transfers between devices, per_device(): lax.psum_scatter(spread_model, 'wsh', scatter_dimension=2, tiled=True)  57 us
  transfers between devices with their start and end apart: 11, of which 10 were waited for; matrix products, arithmetic and copies ran while one was open for 8% of the time, Pallas kernels for 0%

commit v1 on v0

--- a/solution.py
+++ b/solution.py
@@ -1,3 +1,4 @@
+import functools
 import jax
 import jax.numpy as jnp
 from jax import lax
@@ -11,6 +12,23 @@
 NORM_EPS = 1e-06
 ADAPTER_SCALE = 4.0
 ROPE_BASE = 500000.0
+
+
+def works_switch(inner_x, array_axis):
+    plain, near, front = (lax.psum(1, "wsh"), lax.axis_index("wsh"), inner_x.shape[array_axis])
+    fields = [dd * plain if w == array_axis else dd for w, dd in enumerate(inner_x.shape)]
+    kept_arr = lax.dynamic_update_slice_in_dim(
+        jnp.zeros(fields, inner_x.dtype), inner_x, near * front, axis=array_axis
+    )
+    for ix in range(1, plain):
+        inner_x = lax.ppermute(inner_x, "wsh", [(w, (w + 1) % plain) for w in range(plain)])
+        kept_arr = lax.dynamic_update_slice_in_dim(
+            kept_arr, inner_x, (near - ix) % plain * front, axis=array_axis
+        )
+    return kept_arr
+
+
+bring_shapes = functools.partial(works_switch, array_axis=2)
 
 
 def rms_scale(values):
@@ -185,7 +203,7 @@
         )
         return (gate_part, up_part)
 
-    weight_piece = lax.all_gather(mlp_weight, "wsh", axis=2, tiled=True)
+    weight_piece = bring_shapes(mlp_weight)
     adapt_piece = lax.all_gather(adapt_hidden, "wsh", axis=2, tiled=True)
     gathered_rows = pick_rows(adapt_piece, onehot, adapters)
     gate_part, up_part = gate_up_parts(weight_piece, gathered_rows)

time: 1720 us -> 2390 us (1.39)
  waiting for transfers between devices: 1390 us -> 1900 us
  local copies, waits for them, and re-layouts: 42.7 us -> 167 us
  matrix products: 217 us -> 248 us
    ppermute x0 -> x3, waiting for transfers between devices: none -> 1210 us  [works_switch(): lax.ppermute(inner_x, 'wsh', [(w, (w + 1) % plain) for w in range(plain)])]
    all_gather x1, waiting for transfers between devices: 566 us -> 0.01 us  [per_device(): weight_piece = lax.all_gather(mlp_weight, 'wsh', axis=2, tiled=True)]
    dynamic_update_slice x0 -> x4, local copies, waits for them, and re-layouts: none -> 83.9 us  [the longest x3 62.9 us: works_switch(): lax.dynamic_update_slice_in_dim(kept_arr, inner_x, (near - ix) % plain *...]
    all_gather x1, waiting for transfers between devices: 67.9 us -> 0.01 us  [per_device(): lax.all_gather(own_keys, 'ctx', axis=0, tiled=True)]
    all_gather x1, waiting for transfers between devices: 67.7 us -> 0.02 us  [per_device(): lax.all_gather(own_values, 'ctx', axis=0, tiled=True)]
    broadcast_in_dim x0 -> x1, local copies, waits for them, and re-layouts: none -> 31 us  [works_switch(): jnp.zeros(fields, inner_x.dtype)]
  transfers between devices with their start and end apart: 11 -> 14, of which waited for: 10 -> 10; matrix products, arithmetic and copies ran while one was open for 8% -> 13% of each run, Pallas kernels for 0% -> 0%
where the time goes in v1:
time: 2390 us; the launch traced here: 2380 us
  waiting for transfers between devices  1900 us (79%)
  matrix products  248 us (10%)
  local copies, waits for them, and re-layouts  167 us (7%)
  other arithmetic  35.2 us (1%)
    ppermute x3, waiting for transfers between devices, works_switch(): lax.ppermute(inner_x, 'wsh', [(w, (w + 1) % plain) for w in range(plain)])  1210 us
    all_gather x1, waiting for transfers between devices, per_device(): lax.all_gather(attn_weight, 'wsh', axis=2, tiled=True)  197 us
    reduce_scatter x1, waiting for transfers between devices, per_device(): lax.psum_scatter(value_full, 'ctx', scatter_dimension=0, tiled=True)  133 us
    reduce_scatter x1, waiting for transfers between devices, per_device(): lax.psum_scatter(key_full, 'ctx', scatter_dimension=0, tiled=True)  123 us
    psum x1, waiting for transfers between devices, per_device(): model_grads, hidden_grads_out = lax.psum((shard_model, shard_hidden), 'ctx')  117 us
    dynamic_update_slice x3, local copies, waits for them, and re-layouts, works_switch(): lax.dynamic_update_slice_in_dim(kept_arr, inner_x, (near - ix) % plain *...  62.9 us
    reduce_scatter x1, waiting for transfers between devices, per_device(): lax.psum_scatter(spread_model, 'wsh', scatter_dimension=2, tiled=True)  56.9 us
    reduce_scatter x1, waiting for transfers between devices, per_device(): lax.psum_scatter(spread_hidden, 'wsh', scatter_dimension=2, tiled=True)  49.4 us
  transfers between devices with their start and end apart: 14, of which 10 were waited for; matrix products, arithmetic and copies ran while one was open for 13% of the time, Pallas kernels for 0%

profile of v1, /device:TPU:0, one launch (start us, length us, event | category | flops | bytes accessed | tf_op | source)
XLA Modules:
  0.0 2375.4 jit_solution(6121161852607560589)
XLA Ops:
  7.9 11.5 copy.32
  20.3 6.4 all_gather.25
  30.4 9.0 all-gather.10.cloned.1.call-done
  39.4 4.8 fusion.23
  45.8 196.8 %all-gather.8.cloned.1.call-done = bf16[4,2048,2048]{1,2,0:T(8,128)(2,1)} async-done(((bf16[4,2048,512]{1,2,0:T(8,128)(2,1)}), bf16[4,2048,2048]{1,2,0:T(8,128)(2,1)}) %all-gather.8.cloned.1.call-update) | async-done | bytes 33554448 | tf_op jit(solution)/shard_map/all_gather | solution.py:133
  242.6 11.9 fusion.79
  257.7 2.7 copy.35
  272.2 435.0 %collective-permute-done = bf16[3,2048,2048]{2,1,0:T(8,128)(2,1)S(1)} collective-permute-done((bf16[3,2048,2048]{2,1,0:T(8,128)(2,1)}, bf16[3,2048,2048]{2,1,0:T(8,128)(2,1)S(1)}, u32[]{:S(2)}, u32[]{:S(2)}) %collective-permute-start) | collective-permute-done | bytes 25165856 | tf_op jit(solution)/shard_map/ppermute | solution.py:24
  707.2 8.3 copy-done.4
  715.5 638.3 %collective-permute-done.1 = bf16[3,2048,2048]{2,1,0:T(8,128)(2,1)} collective-permute-done((bf16[3,2048,2048]{2,1,0:T(8,128)(2,1)S(1)}, bf16[3,2048,2048]{2,1,0:T(8,128)(2,1)}, u32[]{:S(2)}, u32[]{:S(2)}) %collective-permute-start.1) | collective-permute-done | bytes 25165856 | tf_op jit(solution)/shard_map/ppermute | solution.py:24
  1355.2 31.0 %broadcast_in_dim.30 = bf16[3,2048,8192]{2,1,0:T(8,128)(2,1)} broadcast(bf16[]{:T(256)} %constant.91.clone.1), dimensions={} | broadcast | bytes 100663296 | tf_op jit(solution)/shard_map/broadcast_in_dim | solution.py:21
  1386.2 21.0 constant_dynamic-update-slice_fusion.3
  1407.1 6.6 fusion.21
  1414.6 20.9 constant_dynamic-update-slice_fusion.2
  1435.6 21.0 constant_dynamic-update-slice_fusion.1
  1456.6 4.3 fusion.18
  1464.3 7.2 convolution_convert_fusion
  1471.7 6.4 fusion.17
  1480.1 2.8 convolution_multiply_fusion.1
  1483.0 2.7 convolution_multiply_fusion
  1485.6 141.6 %collective-permute-done.2 = bf16[3,2048,2048]{2,1,0:T(8,128)(2,1)} collective-permute-done((bf16[3,2048,2048]{2,1,0:T(8,128)(2,1)}, bf16[3,2048,2048]{2,1,0:T(8,128)(2,1)}, u32[]{:S(2)}, u32[]{:S(2)}) %collective-permute-start.2) | collective-permute-done | bytes 25165856 | tf_op jit(solution)/shard_map/ppermute | solution.py:24
  1627.2 20.9 constant_dynamic-update-slice_fusion
  1648.2 16.2 fusion.12
  1664.4 15.1 multiply_convert_fusion.4
  1681.8 19.3 fusion.59
  1703.1 15.0 fusion
  1718.1 4.9 convolution_add_fusion
  1723.1 16.2 fusion.11
  1739.2 18.7 multiply_convert_fusion.3
  1759.3 17.0 fusion.4
  1776.3 16.3 fusion.41
  1796.6 4.7 fusion.16
  1802.8 8.2 multiply_reduce_fusion
  1813.5 4.7 broadcast_multiply_fusion
  1818.3 9.4 fusion.86
  1831.4 3.5 convolution_bitcast_fusion
  1835.0 3.4 bitcast_multiply_fusion
  1838.4 4.8 fusion.49
  1843.2 123.0 %reduce-scatter.5.cloned.1.call-done = f32[128,2048]{0,1:T(8,128)} async-done(((f32[1024,2048]{0,1:T(8,128)}), f32[128,2048]{0,1:T(8,128)}) %reduce-scatter.5.cloned.1.call-update) | async-done | bytes 1048592 | tf_op jit(solution)/shard_map/reduce_scatter | solution.py:329
  1973.3 2.7 copy.46
  1976.0 3.0 pad_maximum_fusion.2
  1983.5 133.3 %reduce-scatter.7.cloned.1.call-done = f32[128,2048]{0,1:T(8,128)} async-done(((f32[1024,2048]{0,1:T(8,128)}), f32[128,2048]{0,1:T(8,128)}) %reduce-scatter.7.cloned.1.call-update) | async-done | bytes 1048592 | tf_op jit(solution)/shard_map/reduce_scatter | solution.py:330
  2123.7 3.3 bitcast_multiply_fusion.1
  2127.1 49.4 %reduce-scatter.11.cloned.1.call-done = f32[3,64,2048]{2,1,0:T(8,128)} async-done(((f32[3,64,8192]{2,1,0:T(8,128)}), f32[3,64,2048]{2,1,0:T(8,128)}) %reduce-scatter.11.cloned.1.call-update) | async-done | bytes 1572880 | tf_op jit(solution)/shard_map/reduce_scatter | solution.py:377
  2176.5 56.9 %reduce-scatter.9.cloned.1.call-done = f32[11,64,512]{2,1,0:T(8,128)} async-done(((f32[11,64,2048]{2,1,0:T(8,128)}), f32[11,64,512]{2,1,0:T(8,128)}) %reduce-scatter.9.cloned.1.call-update) | async-done | bytes 1441808 | tf_op jit(solution)/shard_map/reduce_scatter | solution.py:376
  2234.7 11.3 fusion.35
  2246.0 117.4 %all-reduce.3.cloned.1.call-done = (f32[11,64,512]{2,1,0:T(8,128)}, f32[3,64,2048]{2,1,0:T(8,128)}) async-done(((f32[11,64,512]{2,1,0:T(8,128)}, f32[3,64,2048]{2,1,0:T(8,128)}), (f32[11,64,512]{2,1,0:T(8,128)}, f32[3,64,2048]{2,1,0:T(8,128)})) %all-reduce.3.cloned.1.call-update) | async-done | bytes 3014672 | tf_op jit(solution)/shard_map/psum | solution.py:379
  2366.0 2.7 copy.91
  (257 shorter events, 68.6 us)
Async XLA Ops:
  7.2 32.2 %all-gather.10.cloned.1.call-start = ((), (), s32[]{:S(2)}) async-start(), calls=%async_computation.5 | async-start | bytes 3604480 | tf_op jit(solution)/shard_map/all_gather | solution.py:135
  7.9 234.7 %all-gather.8.cloned.1.call-start = ((), (), s32[]{:S(2)}) async-start(), calls=%async_computation.4 | async-start | bytes 41943040 | tf_op jit(solution)/shard_map/all_gather | solution.py:133
  19.5 9.9 copy-start.73
  19.5 1387.6 %all-gather.14.cloned.1.call-start = ((), (), s32[]{:S(2)}) async-start(), calls=%async_computation.7 | async-start | bytes 3932160 | tf_op jit(solution)/shard_map/all_gather | solution.py:207
  20.2 1436.4 %all-gather.12.cloned.1.call-start = ((), (), s32[]{:S(2)}) async-start(), calls=%async_computation.6 | async-start | bytes 4718592 | tf_op jit(solution)/shard_map/all_gather | solution.py:158
  27.3 236.5 %copy-start.47 = (f32[1,2048]{1,0:T(1,128)}, f32[1,2048]{1,0:T(1,128)S(1)}, u32[]{:S(2)}) copy-start(f32[1,2048]{1,0:T(1,128)S(1)} %get-tuple-element.39) | copy-start | bytes 24580
  27.3 237.9 %copy-start.45 = (f32[1,2048]{1,0:T(1,128)}, f32[1,2048]{1,0:T(1,128)S(1)}, u32[]{:S(2)}) copy-start(f32[1,2048]{1,0:T(1,128)S(1)} %get-tuple-element.38) | copy-start | bytes 24580
  27.3 1451.8 %copy-start.49 = (f32[1,2048]{1,0:T(1,128)}, f32[1,2048]{1,0:T(1,128)S(1)}, u32[]{:S(2)}) copy-start(f32[1,2048]{1,0:T(1,128)S(1)} %get-tuple-element.37) | copy-start | bytes 24580
  30.3 235.1 %copy-start.33 = (f32[128,64]{1,0:T(8,128)}, f32[128,64]{1,0:T(8,128)S(1)}, u32[]{:S(2)}) copy-start(f32[128,64]{1,0:T(8,128)S(1)} %get-tuple-element.40) | copy-start | bytes 98308
  30.3 235.1 %copy-start.35 = (f32[128,64]{1,0:T(8,128)}, f32[128,64]{1,0:T(8,128)S(1)}, u32[]{:S(2)}) copy-start(f32[128,64]{1,0:T(8,128)S(1)} %get-tuple-element.41) | copy-start | bytes 98308
  45.8 208.7 %copy-start.54 = (bf16[3,16,128]{2,1,0:T(8,128)(2,1)}, bf16[3,16,128]{2,1,0:T(8,128)(2,1)S(1)}, u32[]{:S(2)}) copy-start(bf16[3,16,128]{2,1,0:T(8,128)(2,1)S(1)} %convolution_convert_fusion.1) | copy-start | bytes 36868
  256.1 14.2 copy-start.1
  270.3 1194.0 %all-gather.18.cloned.1.call-start = ((), (), s32[]{:S(2)}) async-start(), calls=%async_computation.13 | async-start | bytes 4718592 | tf_op jit(solution)/shard_map/all_gather | solution.py:159
  271.2 1431.9 %all-gather.16.cloned.1.call-start = ((), (), s32[]{:S(2)}) async-start(), calls=%async_computation.8 | async-start | bytes 125829120 | tf_op jit(solution)/shard_map/all_gather | solution.py:237
  271.8 1694.4 %reduce-scatter.5.cloned.1.call-start = ((), (), s32[]{:S(2)}) async-start(), calls=%async_computation.9 | async-start | bytes 9437184 | tf_op jit(solution)/shard_map/reduce_scatter | solution.py:329
  271.9 435.3 %collective-permute-start = (bf16[3,2048,2048]{2,1,0:T(8,128)(2,1)}, bf16[3,2048,2048]{2,1,0:T(8,128)(2,1)S(1)}, u32[]{:S(2)}, u32[]{:S(2)}) collective-permute-start(bf16[3,2048,2048]{2,1,0:T(8,128)(2,1)} %param.13), channel_id=1, source_target_pairs={{0,1},{1,2},{2,3},{3,0},{4,5},{5,6},{6,7},{7,4},{8,9},{9,10},{10,1... | collective-permute-start | bytes 75497480 | tf_op jit(solution)/shard_map/ppermute | solution.py:24
  707.2 8.3 copy-start.4
  715.5 638.3 %collective-permute-start.1 = (bf16[3,2048,2048]{2,1,0:T(8,128)(2,1)S(1)}, bf16[3,2048,2048]{2,1,0:T(8,128)(2,1)}, u32[]{:S(2)}, u32[]{:S(2)}) collective-permute-start(bf16[3,2048,2048]{2,1,0:T(8,128)(2,1)S(1)} %collective-permute-done), channel_id=1, source_target_pairs={{0,1},{1,2},{2,3},{3,0},{4,5},{5,6},{6,7},{7,4},{8,9},{9,10},{10,1... | collective-permute-start | bytes 75497480 | tf_op jit(solution)/shard_map/ppermute | solution.py:24
  1353.8 273.4 %collective-permute-start.2 = (bf16[3,2048,2048]{2,1,0:T(8,128)(2,1)}, bf16[3,2048,2048]{2,1,0:T(8,128)(2,1)}, u32[]{:S(2)}, u32[]{:S(2)}) collective-permute-start(bf16[3,2048,2048]{2,1,0:T(8,128)(2,1)} %collective-permute-done.1), channel_id=1, source_target_pairs={{0,1},{1,2},{2,3},{3,0},{4,5},{5,6},{6,7},{7,4},{8,9},{9,10},{10,1... | collective-permute-start | bytes 75497480 | tf_op jit(solution)/shard_map/ppermute | solution.py:24
  1355.1 109.1 %copy-start.14 = (pred[128,1024]{1,0:T(8,128)(4,1)}, pred[128,1024]{1,0:T(8,128)(4,1)S(1)}, u32[]{:S(2)}) copy-start(pred[128,1024]{1,0:T(8,128)(4,1)S(1)} %compare_and_fusion) | copy-start | bytes 393220
  1435.5 21.0 copy-start.22
  1435.5 21.0 copy-start.24
  1479.8 259.4 %copy-start.16 = (bf16[128,2048]{1,0:T(8,128)(2,1)}, bf16[128,2048]{1,0:T(8,128)(2,1)S(1)}, u32[]{:S(2)}) copy-start(bf16[128,2048]{1,0:T(8,128)(2,1)S(1)} %fusion.73) | copy-start | bytes 1572868
  1664.4 17.4 copy-start.53
  1664.4 17.4 copy-start.67
  1681.5 19.6 copy-start.58
  1702.8 15.3 copy-start.18
  1776.3 16.4 copy-start.6
  1776.3 16.4 copy-start.50
  1776.3 17.7 copy-start.9
  1776.3 17.7 copy-start.27
  1776.3 17.8 copy-start.66
  1776.3 17.8 copy-start.70
  1802.7 8.2 slice-start
  1818.3 298.5 %reduce-scatter.7.cloned.1.call-start = ((), (), s32[]{:S(2)}) async-start(), calls=%async_computation.10 | async-start | bytes 9437184 | tf_op jit(solution)/shard_map/reduce_scatter | solution.py:330
  1827.8 348.7 %reduce-scatter.11.cloned.1.call-start = ((), (), s32[]{:S(2)}) async-start(), calls=%async_computation.12 | async-start | bytes 7864320 | tf_op jit(solution)/shard_map/reduce_scatter | solution.py:377
  1838.4 395.1 %reduce-scatter.9.cloned.1.call-start = ((), (), s32[]{:S(2)}) async-start(), calls=%async_computation.11 | async-start | bytes 7208960 | tf_op jit(solution)/shard_map/reduce_scatter | solution.py:376
  1843.2 126.8 %copy-start.34 = (f32[128,64]{1,0:T(8,128)S(1)}, f32[128,64]{1,0:T(8,128)}, u32[]{:S(2)}) copy-start(f32[128,64]{1,0:T(8,128)} %copy-done.33) | copy-start | bytes 98308
  1843.2 126.8 %copy-start.36 = (f32[128,64]{1,0:T(8,128)S(1)}, f32[128,64]{1,0:T(8,128)}, u32[]{:S(2)}) copy-start(f32[128,64]{1,0:T(8,128)} %copy-done.35) | copy-start | bytes 98308
  1979.0 139.1 %copy-start.61 = (f32[128]{0:T(128)S(1)}, f32[128]{0:T(128)}, u32[]{:S(2)}) copy-start(f32[128]{0:T(128)} %copy-done.60) | copy-start | bytes 1540
  1979.0 139.1 %copy-start.63 = (f32[128]{0:T(128)S(1)}, f32[128]{0:T(128)}, u32[]{:S(2)}) copy-start(f32[128]{0:T(128)} %copy-done.62) | copy-start | bytes 1540
  1979.0 139.1 %copy-start.68 = (f32[128]{0:T(128)S(1)}, f32[128]{0:T(128)}, u32[]{:S(2)}) copy-start(f32[128]{0:T(128)} %get-tuple-element.44) | copy-start | bytes 1540
  1979.0 139.1 %copy-start.69 = (f32[128]{0:T(128)S(1)}, f32[128]{0:T(128)}, u32[]{:S(2)}) copy-start(f32[128]{0:T(128)} %get-tuple-element.61) | copy-start | bytes 1540
  2127.0 107.7 %copy-start.29 = (f32[128,2048]{1,0:T(8,128)S(1)}, f32[128,2048]{1,0:T(8,128)}, u32[]{:S(2)}) copy-start(f32[128,2048]{1,0:T(8,128)} %copy-done.28) | copy-start | bytes 3145732
  2127.0 107.7 %copy-start.38 = (bf16[1,128,2048]{1,2,0:T(8,128)(2,1)S(1)}, bf16[1,128,2048]{1,2,0:T(8,128)(2,1)}, u32[]{:S(2)}) copy-start(bf16[1,128,2048]{1,2,0:T(8,128)(2,1)} %copy-done.37) | copy-start | bytes 1572868
  2127.0 107.7 %copy-start.40 = (bf16[1,128,2048]{1,2,0:T(8,128)(2,1)S(1)}, bf16[1,128,2048]{1,2,0:T(8,128)(2,1)}, u32[]{:S(2)}) copy-start(bf16[1,128,2048]{1,2,0:T(8,128)(2,1)} %copy-done.39) | copy-start | bytes 1572868
  2127.0 107.7 %copy-start.42 = (bf16[1,128,2048]{1,2,0:T(8,128)(2,1)S(1)}, bf16[1,128,2048]{1,2,0:T(8,128)(2,1)}, u32[]{:S(2)}) copy-start(bf16[1,128,2048]{1,2,0:T(8,128)(2,1)} %copy-done.41) | copy-start | bytes 1572868
  2127.0 236.4 %all-reduce.3.cloned.1.call-start = ((), (), s32[]{:S(2)}) async-start(), calls=%async_computation.14 | async-start | bytes 6029312 | tf_op jit(solution)/shard_map/psum | solution.py:379
  (43 other events, 187.2 us)
Sparse Core Ops, SparseCore 0:
  9.5 29.8 all-gather.9
  41.0 201.5 all-gather.7
  244.2 28.4 all-gather.13
  275.2 74.6 all-gather.11
  352.3 72.8 all-gather.17
  426.6 846.1 all-gather.15
  1818.4 147.7 reduce-scatter.4
  1969.8 146.9 reduce-scatter.6
  2119.4 57.0 reduce-scatter.10
  2178.9 54.5 reduce-scatter.8
  2237.2 126.1 all-reduce.2
